TPU v7x, 32 devices: a whole 2x2x4 slice. The times are simulated.
32 devices in a mesh: pair: 8 (over z, x), rows: 4 (over y, core).
Axes of the slice: x: 2, y: 2, z: 4, core: 2. Of those that a mesh axis runs over, the one named last changes fastest.
Arguments:
- matrix: float32 [16384, 2048], P('rows', 'pair')
- plan: int32 [3, 8], P(None, 'pair'), may hold values 0 or 1
Outputs:
- rotated: float32 [16384, 2048], P('rows', 'pair')
- offness: float32 [3], replicated
All inputs are finite; a program needn't handle non-finite values. No bound on the sum of `plan` on one device may be relied on, other than what follows from the above.
Results may differ from a plain program's by a relative error of at most 0.00025.
Values sent between devices are 32-bit elements; how exact they have to be, the bound alone decides.
A program may use at most 64 MiB of HBM per device.

v0:
```python
import jax
import jax.numpy as jnp
from jax import lax
from jax.sharding import PartitionSpec as P

ROUNDS = 3


def from_behind(x, axis, by):
    peers = lax.axis_size(axis)
    return lax.ppermute(x, axis, [(i, (i + by) % peers) for i in range(peers)])


def off_total(value):
    return lax.psum(value, "pair")


def pass_on(block):
    return from_behind(block, "pair", 1)


def make_rotation(gram, mean_sq, eye, weights):
    diagonal = jnp.diagonal(gram)
    denom = diagonal[:, None] + diagonal[None, :] + mean_sq
    skew = gram * (weights[None, :] - weights[:, None]) / denom
    square = jnp.dot(skew, skew, precision=lax.Precision.HIGHEST)
    plus = eye + skew
    numer = jnp.dot(plus, plus, precision=lax.Precision.HIGHEST)
    lower = jnp.linalg.cholesky(eye - square)
    return jax.scipy.linalg.cho_solve((lower, True), numer)


def local(matrix, plan):
    width = matrix.shape[1]
    half = width // 2
    pair_count = lax.axis_size("pair")
    ncols_all = width * pair_count
    eye = jnp.eye(width, dtype=jnp.float32)
    weights = jnp.arange(width, dtype=jnp.float32) / jnp.float32(width - 1)
    mean_sq = lax.psum(jnp.sum(matrix * matrix), ("pair", "rows")) / ncols_all
    current = matrix
    values = []
    for step in range(ROUNDS):
        partial_gram = lax.dot_general(
            current,
            current,
            (((0,), (0,)), ((), ())),
            precision=lax.Precision.HIGHEST,
            preferred_element_type=jnp.float32,
        )
        gram = lax.psum(partial_gram, "rows")
        offdiag = gram * (1.0 - eye)
        off_local = jnp.sum(offdiag * offdiag)
        if step == 0:
            total_off = off_total(off_local)
        else:
            total_off = off_total(off_local)
        values.append(jnp.sqrt(total_off / (pair_count * width * (width - 1))) / mean_sq)
        rotation = make_rotation(gram, mean_sq, eye, weights)
        keep_last = plan[step, 0] == 1
        turned = jnp.dot(current, rotation, precision=lax.Precision.HIGHEST)
        first_half = turned[:, :half]
        second_half = turned[:, half:]
        kept = jnp.where(keep_last, second_half, first_half)
        moving = jnp.where(keep_last, first_half, second_half)
        arrived = pass_on(moving)
        current = jnp.concatenate([kept, arrived], axis=1)
    return (current, jnp.stack(values))


def solution(mesh):
    in_specs = (P("rows", "pair"), P(None, "pair"))
    out_specs = (P("rows", "pair"), P())
    return jax.shard_map(local, mesh=mesh, in_specs=in_specs, out_specs=out_specs, check_vma=False)
```

profile of v0, /device:TPU:0, one launch (start us, length us, event | category | flops | bytes accessed | tf_op | source)
XLA Modules:
  0.0 539.0 jit_solution(11518162019927558470)
XLA Ops:
  7.2 10.9 %fusion.76 = f32[256,256]{0,1:T(8,128)} fusion(f32[4096,256]{1,0:T(8,128)} %param.5), kind=kOutput, calls=%fused_computation.150 | convolution fusion | flops 3221225472 | bytes 4456448 | tf_op jit(solution)/shard_map/dot_general | solution.py:44
  18.2 3.9 multiply_reduce_fusion
  22.7 42.2 %psum.50 = f32[]{:T(128)} all-reduce(f32[]{:T(128)} %multiply_reduce_fusion), channel_id=1, replica_groups=mesh['pair'=8,'rows'=4] {'pair','rows'}, use_global_device_ids=true, to_apply=%region_2.0 | all-reduce | flops 1 | bytes 8 | tf_op jit(solution)/shard_map/psum | solution.py:40
  66.3 2.7 gather_fusion
  69.0 1.6 convolution_subtract_fusion.2
  70.7 11.7 %cholesky.172 = f32[128,128]{1,0:T(8,128)S(1)} custom-call(f32[128,128]{1,0:T(8,128)S(1)} %cholesky.270), custom_call_target="Cholesky" | custom-call | tf_op jit(solution)/shard_map/jit(cholesky)/cholesky | solution.py:29
  82.5 9.8 %custom-call.23 = f32[1,128,128]{1,2,0:T(8,128)S(1)} custom-call(f32[1,128,128]{2,1,0:T(8,128)S(1)} %get-tuple-element.81), custom_call_target="InvertDiagBlocksLowerTriangular" | custom-call | tf_op jit(solution)/shard_map/jit(cholesky)/cholesky | solution.py:29
  92.8 11.7 %cholesky.189 = f32[128,128]{1,0:T(8,128)S(1)} custom-call(f32[128,128]{1,0:T(8,128)S(1)} %convolution_subtract_fusion.11), custom_call_target="Cholesky" | custom-call | tf_op jit(solution)/shard_map/jit(cholesky)/cholesky | solution.py:29
  106.6 4.0 while.6
  107.2 1.4 bitcast_dynamic-update-slice_fusion.6
  109.2 1.4 bitcast_dynamic-update-slice_fusion.6
  110.6 19.9 %custom-call.24 = f32[2,128,128]{1,2,0:T(8,128)S(1)} custom-call(f32[2,128,128]{2,1,0:T(8,128)S(1)} %get-tuple-element.24), custom_call_target="InvertDiagBlocksLowerTriangular" | custom-call | tf_op jit(solution)/shard_map/jit(_cho_solve)/triangular_solve | solution.py:30
  133.0 8.8 %convolution_bitcast_fusion = f32[4096,256]{0,1:T(8,128)S(1)} fusion(f32[4096,256]{1,0:T(8,128)} %param.5, f32[128,256]{1,0:T(8,128)S(1)} %fusion.47, f32[128,256]{1,0:T(8,128)S(1)} %fusion.46), kind=kOutput, calls=%fused_computation.9 | convolution fusion | flops 3221291008 | bytes 8650752 | tf_op jit(solution)/shard_map/dot_general | solution.py:61
  142.2 2.3 collective-permute-start
  144.5 47.0 %collective-permute-done = f32[4096,128]{0,1:T(8,128)S(1)} collective-permute-done((f32[4096,128]{0,1:T(8,128)S(1)}, f32[4096,128]{0,1:T(8,128)S(1)}, u32[]{:S(2)}, u32[]{:S(2)}) %collective-permute-start) | collective-permute-done | bytes 2097184 | tf_op jit(solution)/shard_map/ppermute | solution.py:11
  191.6 1.3 copy-done.5
  192.9 4.2 fusion.3
  198.2 28.6 %all-reduce.8.cloned.1.call-done = f32[256,256]{0,1:T(8,128)} async-done(((f32[256,256]{0,1:T(8,128)}), f32[256,256]{0,1:T(8,128)}) %all-reduce.8.cloned.1.call-update) | async-done | bytes 262160 | tf_op jit(solution)/shard_map/psum | solution.py:51
  226.8 2.7 gather_fusion.1
  229.4 1.6 convolution_subtract_fusion.1
  231.2 11.7 %cholesky.206 = f32[128,128]{1,0:T(8,128)S(1)} custom-call(f32[128,128]{1,0:T(8,128)S(1)} %cholesky.273), custom_call_target="Cholesky" | custom-call | tf_op jit(solution)/shard_map/jit(cholesky)/cholesky | solution.py:29
  243.7 9.8 %custom-call.25 = f32[1,128,128]{1,2,0:T(8,128)S(1)} custom-call(f32[1,128,128]{2,1,0:T(8,128)S(1)} %get-tuple-element.77), custom_call_target="InvertDiagBlocksLowerTriangular" | custom-call | tf_op jit(solution)/shard_map/jit(cholesky)/cholesky | solution.py:29
  254.0 11.7 %cholesky.223 = f32[128,128]{1,0:T(8,128)S(1)} custom-call(f32[128,128]{1,0:T(8,128)S(1)} %convolution_subtract_fusion.10), custom_call_target="Cholesky" | custom-call | tf_op jit(solution)/shard_map/jit(cholesky)/cholesky | solution.py:29
  267.8 4.2 while.7
  268.6 1.3 bitcast_dynamic-update-slice_fusion.7
  270.6 1.3 bitcast_dynamic-update-slice_fusion.7
  272.0 19.7 %custom-call.26 = f32[2,128,128]{1,2,0:T(8,128)S(1)} custom-call(f32[2,128,128]{2,1,0:T(8,128)S(1)} %get-tuple-element.25), custom_call_target="InvertDiagBlocksLowerTriangular" | custom-call | tf_op jit(solution)/shard_map/jit(_cho_solve)/triangular_solve | solution.py:30
  294.2 4.0 fusion.2
  298.6 1.7 collective-permute-start.1
  300.3 47.2 %collective-permute-done.1 = f32[4096,128]{0,1:T(8,128)S(1)} collective-permute-done((f32[4096,128]{0,1:T(8,128)S(1)}, f32[4096,128]{0,1:T(8,128)S(1)}, u32[]{:S(2)}, u32[]{:S(2)}) %collective-permute-start.1) | collective-permute-done | bytes 2097184 | tf_op jit(solution)/shard_map/ppermute | solution.py:11
  347.6 1.3 copy-done.3
  348.9 4.2 fusion.1
  353.7 29.9 %all-reduce.10.cloned.1.call-done = f32[256,256]{0,1:T(8,128)} async-done(((f32[256,256]{0,1:T(8,128)}), f32[256,256]{0,1:T(8,128)}) %all-reduce.10.cloned.1.call-update) | async-done | bytes 262160 | tf_op jit(solution)/shard_map/psum | solution.py:51
  383.6 2.7 gather_fusion.2
  386.3 1.6 convolution_subtract_fusion
  388.7 11.7 %cholesky.240 = f32[128,128]{1,0:T(8,128)S(1)} custom-call(f32[128,128]{1,0:T(8,128)S(1)} %cholesky.276), custom_call_target="Cholesky" | custom-call | tf_op jit(solution)/shard_map/jit(cholesky)/cholesky | solution.py:29
  401.1 9.8 %custom-call.27 = f32[1,128,128]{1,2,0:T(8,128)S(1)} custom-call(f32[1,128,128]{2,1,0:T(8,128)S(1)} %get-tuple-element.73), custom_call_target="InvertDiagBlocksLowerTriangular" | custom-call | tf_op jit(solution)/shard_map/jit(cholesky)/cholesky | solution.py:29
  413.1 11.9 %cholesky.257 = f32[128,128]{1,0:T(8,128)S(1)} custom-call(f32[128,128]{1,0:T(8,128)S(1)} %convolution_subtract_fusion.9), custom_call_target="Cholesky" | custom-call | tf_op jit(solution)/shard_map/jit(cholesky)/cholesky | solution.py:29
  427.0 3.8 while.8
  427.6 1.3 bitcast_dynamic-update-slice_fusion.8
  429.5 1.3 bitcast_dynamic-update-slice_fusion.8
  430.9 19.7 %custom-call.28 = f32[2,128,128]{1,2,0:T(8,128)S(1)} custom-call(f32[2,128,128]{2,1,0:T(8,128)S(1)} %get-tuple-element.26), custom_call_target="InvertDiagBlocksLowerTriangular" | custom-call | tf_op jit(solution)/shard_map/jit(_cho_solve)/triangular_solve | solution.py:30
  453.1 4.0 fusion
  457.1 1.7 slice_select_fusion.1
  458.8 1.5 collective-permute-start.2
  462.3 57.4 %all-reduce.1 = (f32[]{:T(128)}, f32[]{:T(128)}, f32[]{:T(128)}) all-reduce(f32[]{:T(128)} %fusion.12, f32[]{:T(128)} %fusion.10, f32[]{:T(128)} %fusion.8), channel_id=1, replica_groups=mesh['pair'=8,'rows'=4] {'pair'}, use_global_device_ids=true, to_apply=%region_14.17 | all-reduce | flops 3 | bytes 24 | tf_op jit(solution)/shard_map/psum | solution.py:15
  522.5 3.9 pad_maximum_fusion.2
  526.5 5.6 %copy.23 = f32[4096,256]{1,0:T(8,128)} copy(f32[4096,256]{0,1:T(8,128)} %pad_maximum_fusion.2) | data formatting | bytes 8388608
  (103 shorter events, 23.8 us)
Async XLA Ops:
  7.2 59.1 %all-reduce.6.cloned.1.call-start = ((), (), s32[]{:S(2)}) async-start(), calls=%async_computation | async-start | bytes 524288 | tf_op jit(solution)/shard_map/psum | solution.py:51
  18.1 4.0 copy-start.8
  18.1 208.7 %all-reduce.8.cloned.1.call-start = ((), (), s32[]{:S(2)}) async-start(), calls=%async_computation.1 | async-start | bytes 524288 | tf_op jit(solution)/shard_map/psum | solution.py:51
  66.3 64.2 %copy-start = (f32[256,256]{0,1:T(8,128)S(1)}, f32[256,256]{0,1:T(8,128)}, u32[]{:S(2)}) copy-start(f32[256,256]{0,1:T(8,128)} %all-reduce.6.cloned.1.call-done) | copy-start | bytes 786436
  142.2 49.4 %collective-permute-start = (f32[4096,128]{0,1:T(8,128)S(1)}, f32[4096,128]{0,1:T(8,128)S(1)}, u32[]{:S(2)}, u32[]{:S(2)}) collective-permute-start(f32[4096,128]{0,1:T(8,128)S(1)} %get-tuple-element.69), channel_id=1, source_target_pairs={{0,4},{4,8},{8,12},{12,16},{16,20},{20,24},{24,28},{28,0},{1,5},{5... | collective-permute-start | bytes 6291464 | tf_op jit(solution)/shard_map/ppermute | solution.py:11
  191.5 1.3 copy-start.5
  197.1 186.5 %all-reduce.10.cloned.1.call-start = ((), (), s32[]{:S(2)}) async-start(), calls=%async_computation.2 | async-start | bytes 524288 | tf_op jit(solution)/shard_map/psum | solution.py:51
  226.8 64.9 %copy-start.1 = (f32[256,256]{0,1:T(8,128)S(1)}, f32[256,256]{0,1:T(8,128)}, u32[]{:S(2)}) copy-start(f32[256,256]{0,1:T(8,128)} %all-reduce.8.cloned.1.call-done) | copy-start | bytes 786436
  291.7 2.5 copy-start.6
  298.6 49.0 %collective-permute-start.1 = (f32[4096,128]{0,1:T(8,128)S(1)}, f32[4096,128]{0,1:T(8,128)S(1)}, u32[]{:S(2)}, u32[]{:S(2)}) collective-permute-start(f32[4096,128]{0,1:T(8,128)S(1)} %get-tuple-element.67), channel_id=1, source_target_pairs={{0,4},{4,8},{8,12},{12,16},{16,20},{20,24},{24,28},{28,0},{1,5},{5... | collective-permute-start | bytes 6291464 | tf_op jit(solution)/shard_map/ppermute | solution.py:11
  347.6 1.3 copy-start.3
  383.6 66.9 %copy-start.2 = (f32[256,256]{0,1:T(8,128)S(1)}, f32[256,256]{0,1:T(8,128)}, u32[]{:S(2)}) copy-start(f32[256,256]{0,1:T(8,128)} %all-reduce.10.cloned.1.call-done) | copy-start | bytes 786436
  388.0 0.7 copy-start.7
  450.5 2.5 copy-start.4
  458.8 63.7 %collective-permute-start.2 = (f32[4096,128]{0,1:T(8,128)}, f32[4096,128]{0,1:T(8,128)}, u32[]{:S(2)}, u32[]{:S(2)}) collective-permute-start(f32[4096,128]{0,1:T(8,128)} %get-tuple-element.65), channel_id=1, source_target_pairs={{0,4},{4,8},{8,12},{12,16},{16,20},{20,24},{24,28},{28,0},{1,5},{5... | collective-permute-start | bytes 6291464 | tf_op jit(solution)/shard_map/ppermute | solution.py:11
Sparse Core Ops, SparseCore 0:
  18.2 35.0 all-reduce.5
  197.2 29.4 all-reduce.7
  353.3 30.3 all-reduce.9
where the time goes:
time: 546 us; the launch traced here: 539 us
  other arithmetic  176 us (32%)
  waiting for transfers between devices  153 us (28%)
  blocking collectives  99.7 us (18%)
  matrix products  51.3 us (9%)
  local copies, waits for them, and re-layouts  29.9 us (5%)
  between operations  23.2 us (4%)
  starting transfers between devices  6.06 us (1%)
    another operation x20, other arithmetic, make_rotation(): lower = jnp.linalg.cholesky(eye - square)  103 us
    ppermute x3, waiting for transfers between devices, from_behind(): return lax.ppermute(x, axis, [(i, (i + by) % peers) for i in range(peers)])  94.3 us
    another operation x7, other arithmetic, make_rotation(): return jax.scipy.linalg.cho_solve((lower, True), numer)  59.3 us
    psum x3, waiting for transfers between devices, local(): gram = lax.psum(partial_gram, 'rows')  58.5 us
    psum x1, blocking collectives, off_total(): return lax.psum(value, 'pair')  57.4 us
    psum x1, blocking collectives, local(): mean_sq = lax.psum(jnp.sum(matrix * matrix), ('pair', 'rows')) / ncols_all  42.2 us
    dot_general x3, matrix products, local(): lax.dot_general(current, current, (((0,), (0,)), ((), ())), precision=lax...  19.4 us
    dot_general x3, matrix products, local(): turned = jnp.dot(current, rotation, precision=lax.Precision.HIGHEST)  16.8 us
  transfers between devices with their start and end apart: 6, of which 4 were waited for; matrix products, arithmetic and copies ran while one was open for 1% of the time, Pallas kernels for 0%

commit v1 on v0

v1 whole, which is shorter than its diff:
```python
import functools

import jax
import jax.numpy as jnp
from jax import lax
from jax.experimental import pallas as pl
from jax.experimental.pallas import tpu as pltpu
from jax.sharding import PartitionSpec as P

ROUNDS = 3
CHUNKS = 8
STEPS = 7
MESH = pl.DeviceIdType.MESH
F32 = jnp.float32
BF16 = jnp.bfloat16


def split(x):
    high = x.astype(BF16)
    return high, (x - high.astype(F32)).astype(BF16)


def dot(a, b):
    return jnp.dot(a, b, preferred_element_type=F32)


def tdot(a, b):
    return lax.dot_general(a, b, (((0,), (0,)), ((), ())), preferred_element_type=F32)


def full_dot(a, b):
    return jnp.dot(a, b, precision=lax.Precision.HIGHEST, preferred_element_type=F32)


def full_tdot(a, b):
    return lax.dot_general(
        a, b, (((0,), (0,)), ((), ())), precision=lax.Precision.HIGHEST, preferred_element_type=F32
    )


def total(x):
    return jnp.sum(jnp.sum(x, axis=1, keepdims=True), axis=0, keepdims=True)


def scalings(width):
    spread = sum((i - j) ** 2 for i in range(width) for j in range(width)) / (width - 1) ** 2
    top = 1.0 + spread / 8.0
    first = 2.0 / (1.0 + top)
    err = (top - 1.0) / (top + 1.0)
    out = []
    for _ in range(STEPS):
        scale = 2.0 / (2.0 - err * err)
        out.append(scale)
        err = scale - 1.0
    return first, out


def share(axis, peers, tile_ref, slots, send_sems, recv_sems):
    me = lax.axis_index(axis)

    def copy_to(step):
        to = lax.rem(me + step, peers)
        return pltpu.make_async_remote_copy(
            src_ref=tile_ref,
            dst_ref=slots.at[me],
            send_sem=send_sems.at[step],
            recv_sem=recv_sems.at[step],
            device_id={axis: to},
            device_id_type=MESH,
        )

    def start(step, carry):
        copy_to(step).start()
        return carry

    def finish(step, carry):
        copy_to(step).wait()
        return carry

    lax.fori_loop(1, peers, start, 0)

    def done():
        lax.fori_loop(1, peers, finish, 0)
        slots[me] = tile_ref[...]

        def add(i, acc):
            return acc + slots[i]

        return lax.fori_loop(0, peers, add, jnp.zeros(tile_ref.shape, F32))

    return done


def kernel(
    pairs, groups, x_ref, plan_ref, out_ref, off_ref,
    kb, ab, mov, g_ref, acc, q_hi, q_lo, send0, recv0, sendg, recvg, mass_src, mass_in,
    sq_src, sq_rows, sq_tile, sq_pairs, off_tile, off_pairs,
    load_sem, store_sem, move_send, move_recv, ex_send, ex_recv, mass_send, mass_recv,
    sqr_send, sqr_recv, sqp_send, sqp_recv, off_send, off_recv,
):
    rows_all, width = x_ref.shape
    half = width // 2
    rows = rows_all // CHUNKS
    stages = groups.bit_length() - 1
    pair = lax.axis_index("pair")
    group = lax.axis_index("rows")
    after = lax.rem(pair + 1, pairs)

    def at(c):
        return pl.ds(pl.multiple_of(c * rows, rows), rows)

    def load(c, side):
        dst = ab if side else kb
        return pltpu.make_async_copy(
            x_ref.at[at(c), pl.ds(side * half, half)], dst.at[0, at(c)], load_sem.at[side, c]
        )

    def store(c, side):
        src = ab if side else kb
        return pltpu.make_async_copy(
            src.at[ROUNDS, at(c)], out_ref.at[at(c), pl.ds(side * half, half)], store_sem.at[side, c]
        )

    @pl.loop(0, CHUNKS)
    def _(c):
        load(c, 0).start()
        load(c, 1).start()

    barrier = pltpu.get_barrier_semaphore()

    @pl.loop(1, pairs)
    def _(step):
        pl.semaphore_signal(
            barrier, inc=1, device_id={"pair": lax.rem(pair + step, pairs)}, device_id_type=MESH
        )

    @pl.loop(1, groups)
    def _(step):
        pl.semaphore_signal(
            barrier, inc=1, device_id={"rows": lax.rem(group + step, groups)}, device_id_type=MESH
        )

    sq_src[...] = jnp.zeros_like(sq_src)

    @pl.loop(0, CHUNKS)
    def _(c):
        load(c, 0).wait()
        load(c, 1).wait()
        k = kb[0, at(c)]
        m = ab[0, at(c)]
        sq_src[...] += jnp.sum((k * k + m * m).reshape(rows // 8, 8, half), axis=0)

    pl.semaphore_wait(barrier, pairs - 1 + groups - 1)
    rows_done = share("rows", groups, sq_src, sq_rows, sqr_send, sqr_recv)

    g_ref[...] = jnp.zeros_like(g_ref)
    mass_low = jnp.zeros((width, width), F32)

    def first_gram(c, carry):
        high_high, high_low = carry
        high, low = split(jnp.concatenate([kb[0, at(c)], ab[0, at(c)]], axis=1))
        return high_high + tdot(high, high), high_low + tdot(high, low)

    high_high, high_low = lax.fori_loop(0, CHUNKS, first_gram, (mass_low, mass_low))
    gram = high_high + high_low + high_low.T
    send0[0] = jnp.concatenate([gram[:half], gram[half:, half:]], axis=1)

    def swap(send, recv, step, stage):
        return pltpu.make_async_remote_copy(
            src_ref=send.at[stage],
            dst_ref=recv.at[stage],
            send_sem=ex_send.at[step, stage],
            recv_sem=ex_recv.at[step, stage],
            device_id={"rows": jnp.bitwise_xor(group, 1 << stage)},
            device_id_type=MESH,
        )

    def reduce_rows(send, recv, step):
        for stage in range(stages):
            copy = swap(send, recv, step, stage)
            copy.start()
            copy.wait()
            send[stage + 1] = send[stage] + recv[stage]
        return send[stages]

    first_swap = swap(send0, recv0, 0, 0)
    first_swap.start()
    sq_tile[...] = rows_done()
    pairs_done = share("pair", pairs, sq_tile, sq_pairs, sqp_send, sqp_recv)
    first_swap.wait()
    send0[1] = send0[0] + recv0[0]
    for stage in range(1, stages):
        copy = swap(send0, recv0, 0, stage)
        copy.start()
        copy.wait()
        send0[stage + 1] = send0[stage] + recv0[stage]
    gram = send0[stages]
    g_ref[:half, :] = gram[:, :width]
    g_ref[half:, :half] = gram[:, half:width].T
    g_ref[half:, half:] = gram[:, width:]
    mean_sq = total(pairs_done()) / (width * pairs)

    row_id = lax.broadcasted_iota(jnp.int32, (width, width), 0)
    col_id = lax.broadcasted_iota(jnp.int32, (width, width), 1)
    eye = (row_id == col_id).astype(F32)
    off_tile[...] = jnp.zeros_like(off_tile)
    first_scale, scales = scalings(width)

    def move(r, c):
        return pltpu.make_async_remote_copy(
            src_ref=mov.at[r, at(c)],
            dst_ref=ab.at[r + 1, at(c)],
            send_sem=move_send.at[r, c],
            recv_sem=move_recv.at[r, c],
            device_id={"pair": after},
            device_id_type=MESH,
        )

    def pass_mass(r):
        return pltpu.make_async_remote_copy(
            src_ref=mass_src.at[r],
            dst_ref=mass_in.at[r],
            send_sem=mass_send.at[r],
            recv_sem=mass_recv.at[r],
            device_id={"pair": after},
            device_id_type=MESH,
        )

    @pl.loop(0, ROUNDS)
    def _(r):
        gram = g_ref[...]
        diag = gram * eye
        denom = jnp.sum(diag, axis=1, keepdims=True) + jnp.sum(diag, axis=0, keepdims=True) + mean_sq
        weight = (col_id.astype(F32) - row_id.astype(F32)) * F32(1.0 / (width - 1))
        skew = gram * weight / denom
        square = full_dot(skew, skew)
        resid = eye - F32(first_scale) * (eye - square)
        inverse = F32(first_scale) * (eye + skew)

        def refine(i, carry):
            resid, inverse = carry
            scale = F32(scales[0])
            for j in range(1, STEPS - 1):
                scale = jnp.where(i == j, F32(scales[j]), scale)
            inverse = scale * (inverse + full_dot(inverse, resid))
            resid = scale * full_dot(resid, resid) + (1.0 - scale) * eye
            return resid, inverse

        resid, inverse = lax.fori_loop(0, STEPS - 1, refine, (resid, inverse))
        inverse = F32(scales[STEPS - 1]) * (inverse + full_dot(inverse, resid))
        wrong = eye - (inverse - full_dot(skew, inverse))
        inverse = inverse + full_dot(inverse, wrong)
        rotation = 2.0 * inverse - eye
        flag = jnp.full((width, width), plan_ref[r, 0], jnp.int32)
        turned = jnp.concatenate([rotation[:, half:], rotation[:, :half]], axis=1)
        rotation = jnp.where(flag == 1, turned, rotation)
        high, low = split(rotation)
        q_hi[...] = high
        q_lo[...] = low

        @pl.loop(0, CHUNKS)
        def _(c):
            high, low = split(jnp.concatenate([kb[r, at(c)], ab[r, at(c)]], axis=1))
            y = dot(high, q_hi[...]) + (dot(high, q_lo[...]) + dot(low, q_hi[...]))
            mov[r, at(c)] = y[:, half:]
            move(r, c).start()
            kb[r + 1, at(c)] = y[:, :half]

        off = gram * (1.0 - eye)
        tile_row = lax.broadcasted_iota(jnp.int32, off_tile.shape, 0)
        off_tile[...] = jnp.where(tile_row == r, total(off * off), off_tile[...])

        @pl.when(r < ROUNDS - 1)
        def _():
            mass = full_tdot(rotation, full_dot(gram, rotation))
            mass_src[r] = mass[half:, half:]
            pass_mass(r).start()
            g_ref[:half, :half] = mass[:half, :half]
            acc[...] = jnp.zeros_like(acc)

            @pl.loop(0, CHUNKS)
            def _(c):
                k_high, k_low = split(kb[r + 1, at(c)])
                move(r, c).wait()
                m_high, m_low = split(ab[r + 1, at(c)])
                acc[...] += tdot(k_high, m_high) + (tdot(k_high, m_low) + tdot(k_low, m_high))

            sendg[r, 0] = acc[...]
            cross = reduce_rows(sendg.at[r], recvg.at[r], r + 1)
            pass_mass(r).wait()
            g_ref[:half, half:] = cross
            g_ref[half:, :half] = cross.T
            g_ref[half:, half:] = mass_in[r]

    off_done = share("pair", pairs, off_tile, off_pairs, off_send, off_recv)

    @pl.loop(0, CHUNKS)
    def _(c):
        store(c, 0).start()

    off_ref[...] = jnp.sqrt(off_done() / (pairs * width * (width - 1))) / mean_sq

    @pl.loop(0, CHUNKS)
    def _(c):
        move(ROUNDS - 1, c).wait()
        store(c, 1).start()

    @pl.loop(0, CHUNKS)
    def _(c):
        store(c, 0).wait()
        store(c, 1).wait()


def local(matrix, plan):
    rows, width = matrix.shape
    half = width // 2
    pairs = lax.axis_size("pair")
    groups = lax.axis_size("rows")
    if groups & (groups - 1) or rows % (CHUNKS * 8):
        raise ValueError("sizes")
    stages = groups.bit_length() - 1
    dma = pltpu.SemaphoreType.DMA
    tile = (8, 128)
    rotated, off = pl.pallas_call(
        functools.partial(kernel, pairs, groups),
        out_shape=(
            jax.ShapeDtypeStruct(matrix.shape, F32),
            jax.ShapeDtypeStruct(tile, F32),
        ),
        in_specs=[pl.BlockSpec(memory_space=pl.ANY), pl.BlockSpec(memory_space=pltpu.SMEM)],
        out_specs=(pl.BlockSpec(memory_space=pl.ANY), pl.BlockSpec(memory_space=pltpu.VMEM)),
        scratch_shapes=[
            pltpu.VMEM((ROUNDS + 1, rows, half), F32),
            pltpu.VMEM((ROUNDS + 1, rows, half), F32),
            pltpu.VMEM((ROUNDS, rows, half), F32),
            pltpu.VMEM((width, width), F32),
            pltpu.VMEM((half, half), F32),
            pltpu.VMEM((width, width), BF16),
            pltpu.VMEM((width, width), BF16),
            pltpu.VMEM((stages + 1, half, 3 * half), F32),
            pltpu.VMEM((stages, half, 3 * half), F32),
            pltpu.VMEM((ROUNDS, stages + 1, half, half), F32),
            pltpu.VMEM((ROUNDS, stages, half, half), F32),
            pltpu.VMEM((ROUNDS, half, half), F32),
            pltpu.VMEM((ROUNDS, half, half), F32),
            pltpu.VMEM(tile, F32),
            pltpu.VMEM((groups,) + tile, F32),
            pltpu.VMEM(tile, F32),
            pltpu.VMEM((pairs,) + tile, F32),
            pltpu.VMEM(tile, F32),
            pltpu.VMEM((pairs,) + tile, F32),
            dma((2, CHUNKS)),
            dma((2, CHUNKS)),
            dma((ROUNDS, CHUNKS)),
            dma((ROUNDS, CHUNKS)),
            dma((ROUNDS, stages)),
            dma((ROUNDS, stages)),
            dma((ROUNDS,)),
            dma((ROUNDS,)),
            dma((groups,)),
            dma((groups,)),
            dma((pairs,)),
            dma((pairs,)),
            dma((pairs,)),
            dma((pairs,)),
        ],
        compiler_params=pltpu.CompilerParams(
            collective_id=0, has_side_effects=True, vmem_limit_bytes=50 * 2**20
        ),
    )(matrix, plan)
    return rotated, off[:ROUNDS, 0]


def solution(mesh):
    in_specs = (P("rows", "pair"), P(None, "pair"))
    out_specs = (P("rows", "pair"), P())
    return jax.shard_map(local, mesh=mesh, in_specs=in_specs, out_specs=out_specs, check_vma=False)
```

time: 546 us -> 199 us (0.36); the launches traced: 539 us -> 199 us
  Pallas kernels: 0 us -> 192 us
  other arithmetic: 176 us -> 0 us
  waiting for transfers between devices: 153 us -> 0 us
  blocking collectives: 99.7 us -> 0 us
  matrix products: 51.3 us -> 0 us
  local copies, waits for them, and re-layouts: 29.9 us -> 5.84 us
  between operations: 23.2 us -> 0.64 us
  starting transfers between devices: 6.06 us -> 0 us
    pallas_call x0 -> x1, Pallas kernels: none -> 192 us  [local(): pl.pallas_call(functools.partial(kernel, pairs, groups), out_shape=(jax.S...]
    another operation x28 -> x0, other arithmetic: 163 us -> none  [the longest x20 103 us: make_rotation(): lower = jnp.linalg.cholesky(eye - square)]
    psum x2 -> x0, blocking collectives: 99.7 us -> none  [the longest x1 57.4 us: off_total(): return lax.psum(value, 'pair')]
    ppermute x3 -> x0, waiting for transfers between devices: 94.3 us -> none  [from_behind(): return lax.ppermute(x, axis, [(i, (i + by) % peers) for i in range(peers)])]
    psum x3 -> x0, waiting for transfers between devices: 58.5 us -> none  [local(): gram = lax.psum(partial_gram, 'rows')]
    dot_general x12 -> x0, matrix products: 43.1 us -> none  [the longest x3 19.4 us: local(): lax.dot_general(current, current, (((0,), (0,)), ((), ())), precision=lax...]
    another operation x28 -> x0, local copies, waits for them, and re-layouts: 11.9 us -> none  [the longest x22 11.9 us: make_rotation(): return jax.scipy.linalg.cho_solve((lower, True), numer)]
    another operation x24 -> x0, matrix products: 8.22 us -> none  [the longest x18 5.12 us: make_rotation(): return jax.scipy.linalg.cho_solve((lower, True), numer)]
  transfers between devices with their start and end apart: 6 -> 0, of which waited for: 4 -> 0; matrix products, arithmetic and copies ran while one was open for 1% -> 0% of each run, Pallas kernels for 0% -> 0%
where the time goes in v1:
time: 199 us
  Pallas kernels  192 us (96%)
  local copies, waits for them, and re-layouts  5.84 us (3%)
    pallas_call x1, Pallas kernels, local(): pl.pallas_call(functools.partial(kernel, pairs, groups), out_shape=(jax.S...  192 us
    unnamed x2, local copies, waits for them, and re-layouts  5.21 us

profile of v1, /device:TPU:0, one launch (start us, length us, event | category | flops | bytes accessed | tf_op | source)
XLA Modules:
  0.0 198.5 jit_solution(5814265152531163625)
XLA Ops:
  0.6 0.7 copy.5.plan_ref
  1.4 192.0 %shard_map.41 = (f32[4096,256]{1,0:T(8,128)}, f32[8,128]{1,0:T(8,128)S(1)}) custom-call(f32[4096,256]{1,0:T(8,128)} %x_ref.1, s32[3,1]{1,0:T(4,128)S(1)} %copy.5.plan_ref), custom_call_target="tpu_custom_call" | custom-call | tf_op jit(solution)/shard_map/pallas_call | solution.py:324
  193.4 0.6 slice_reduce_fusion
  194.1 4.5 %copy.7 = f32[4096,256]{1,0:T(8,128)} copy(f32[4096,256]{1,0:T(8,128)} %get-tuple-element.8) | data formatting | bytes 8388608

commit v2 on v1

--- a/solution.py
+++ b/solution.py
@@ -8,7 +8,7 @@
 from jax.sharding import PartitionSpec as P
 
 ROUNDS = 3
-CHUNKS = 8
+CHUNKS = 16
 STEPS = 7
 MESH = pl.DeviceIdType.MESH
 F32 = jnp.float32
@@ -30,6 +30,12 @@
 
 def full_dot(a, b):
     return jnp.dot(a, b, precision=lax.Precision.HIGHEST, preferred_element_type=F32)
+
+
+def wide_dot(a, b):
+    a_high, a_low = split(a)
+    b_high, b_low = split(b)
+    return dot(a_high, b_high) + (dot(a_high, b_low) + dot(a_low, b_high))
 
 
 def full_tdot(a, b):
@@ -233,7 +239,7 @@
         denom = jnp.sum(diag, axis=1, keepdims=True) + jnp.sum(diag, axis=0, keepdims=True) + mean_sq
         weight = (col_id.astype(F32) - row_id.astype(F32)) * F32(1.0 / (width - 1))
         skew = gram * weight / denom
-        square = full_dot(skew, skew)
+        square = wide_dot(skew, skew)
         resid = eye - F32(first_scale) * (eye - square)
         inverse = F32(first_scale) * (eye + skew)
 
@@ -242,14 +248,14 @@
             scale = F32(scales[0])
             for j in range(1, STEPS - 1):
                 scale = jnp.where(i == j, F32(scales[j]), scale)
-            inverse = scale * (inverse + full_dot(inverse, resid))
-            resid = scale * full_dot(resid, resid) + (1.0 - scale) * eye
+            inverse = scale * (inverse + wide_dot(inverse, resid))
+            resid = scale * wide_dot(resid, resid) + (1.0 - scale) * eye
             return resid, inverse
 
         resid, inverse = lax.fori_loop(0, STEPS - 1, refine, (resid, inverse))
-        inverse = F32(scales[STEPS - 1]) * (inverse + full_dot(inverse, resid))
+        inverse = F32(scales[STEPS - 1]) * (inverse + wide_dot(inverse, resid))
         wrong = eye - (inverse - full_dot(skew, inverse))
-        inverse = inverse + full_dot(inverse, wrong)
+        inverse = inverse + wide_dot(inverse, wrong)
         rotation = 2.0 * inverse - eye
         flag = jnp.full((width, width), plan_ref[r, 0], jnp.int32)
         turned = jnp.concatenate([rotation[:, half:], rotation[:, :half]], axis=1)

time: 199 us -> 196 us (0.985)
  Pallas kernels: 192 us -> 189 us
    pallas_call x1, Pallas kernels: 192 us -> 189 us  [local(): pl.pallas_call(functools.partial(kernel, pairs, groups), out_shape=(jax.S...]
where the time goes in v2:
time: 196 us
  Pallas kernels  189 us (96%)
  local copies, waits for them, and re-layouts  5.84 us (3%)
    pallas_call x1, Pallas kernels, local(): pl.pallas_call(functools.partial(kernel, pairs, groups), out_shape=(jax.S...  189 us
    unnamed x2, local copies, waits for them, and re-layouts  5.21 us

profile of v2, /device:TPU:0, one launch (start us, length us, event | category | flops | bytes accessed | tf_op | source)
XLA Modules:
  0.0 195.6 jit_solution(7509388891671708903)
XLA Ops:
  0.6 0.7 copy.5.plan_ref
  1.4 189.1 %shard_map.41 = (f32[4096,256]{1,0:T(8,128)}, f32[8,128]{1,0:T(8,128)S(1)}) custom-call(f32[4096,256]{1,0:T(8,128)} %x_ref.1, s32[3,1]{1,0:T(4,128)S(1)} %copy.5.plan_ref), custom_call_target="tpu_custom_call" | custom-call | tf_op jit(solution)/shard_map/pallas_call | solution.py:330
  190.5 0.6 slice_reduce_fusion
  191.1 4.5 %copy.7 = f32[4096,256]{1,0:T(8,128)} copy(f32[4096,256]{1,0:T(8,128)} %get-tuple-element.8) | data formatting | bytes 8388608

commit v3 on v2

--- a/solution.py
+++ b/solution.py
@@ -8,7 +8,8 @@
 from jax.sharding import PartitionSpec as P
 
 ROUNDS = 3
-CHUNKS = 16
+CHUNKS = 8
+RAW_BLOCKS = 2
 STEPS = 7
 MESH = pl.DeviceIdType.MESH
 F32 = jnp.float32
@@ -100,25 +101,35 @@
 def kernel(
     pairs, groups, x_ref, plan_ref, out_ref, off_ref,
     kb, ab, mov, g_ref, acc, q_hi, q_lo, send0, recv0, sendg, recvg, mass_src, mass_in,
-    sq_src, sq_rows, sq_tile, sq_pairs, off_tile, off_pairs,
+    sq_src, sq_rows, sq_tile, sq_pairs, off_tile, off_pairs, raw_in, q_src, q_in,
     load_sem, store_sem, move_send, move_recv, ex_send, ex_recv, mass_send, mass_recv,
     sqr_send, sqr_recv, sqp_send, sqp_recv, off_send, off_recv,
+    raw_send, raw_recv, q_send, q_recv,
 ):
     rows_all, width = x_ref.shape
     half = width // 2
-    rows = rows_all // CHUNKS
+    raw = raw_in.shape[2]
+    rows = (rows_all - raw) // CHUNKS
+    load_rows = rows_all // CHUNKS
+    raw_rows = raw // RAW_BLOCKS
     stages = groups.bit_length() - 1
     pair = lax.axis_index("pair")
     group = lax.axis_index("rows")
     after = lax.rem(pair + 1, pairs)
 
     def at(c):
-        return pl.ds(pl.multiple_of(c * rows, rows), rows)
+        return pl.ds(pl.multiple_of(raw + c * rows, 16), rows)
+
+    def load_at(c):
+        return pl.ds(pl.multiple_of(c * load_rows, load_rows), load_rows)
+
+    def raw_at(c):
+        return pl.ds(pl.multiple_of(c * raw_rows, raw_rows), raw_rows)
 
     def load(c, side):
         dst = ab if side else kb
         return pltpu.make_async_copy(
-            x_ref.at[at(c), pl.ds(side * half, half)], dst.at[0, at(c)], load_sem.at[side, c]
+            x_ref.at[load_at(c), pl.ds(side * half, half)], dst.at[0, load_at(c)], load_sem.at[side, c]
         )
 
     def store(c, side):
@@ -127,6 +138,34 @@
             src.at[ROUNDS, at(c)], out_ref.at[at(c), pl.ds(side * half, half)], store_sem.at[side, c]
         )
 
+    def store_raw(side):
+        src = ab if side else kb
+        where = pl.ds(0, raw)
+        return pltpu.make_async_copy(
+            src.at[ROUNDS, where], out_ref.at[where, pl.ds(side * half, half)], store_sem.at[side, CHUNKS]
+        )
+
+    def pass_raw(r, side):
+        src = ab if side else kb
+        return pltpu.make_async_remote_copy(
+            src_ref=src.at[r, pl.ds(0, raw)],
+            dst_ref=raw_in.at[r, side],
+            send_sem=raw_send.at[r, side],
+            recv_sem=raw_recv.at[r, side],
+            device_id={"pair": after},
+            device_id_type=MESH,
+        )
+
+    def pass_q(r):
+        return pltpu.make_async_remote_copy(
+            src_ref=q_src.at[r],
+            dst_ref=q_in.at[r],
+            send_sem=q_send.at[r],
+            recv_sem=q_recv.at[r],
+            device_id={"pair": after},
+            device_id_type=MESH,
+        )
+
     @pl.loop(0, CHUNKS)
     def _(c):
         load(c, 0).start()
@@ -152,11 +191,13 @@
     def _(c):
         load(c, 0).wait()
         load(c, 1).wait()
-        k = kb[0, at(c)]
-        m = ab[0, at(c)]
-        sq_src[...] += jnp.sum((k * k + m * m).reshape(rows // 8, 8, half), axis=0)
+        k = kb[0, load_at(c)]
+        m = ab[0, load_at(c)]
+        sq_src[...] += jnp.sum((k * k + m * m).reshape(load_rows // 8, 8, half), axis=0)
 
     pl.semaphore_wait(barrier, pairs - 1 + groups - 1)
+    pass_raw(0, 0).start()
+    pass_raw(0, 1).start()
     rows_done = share("rows", groups, sq_src, sq_rows, sqr_send, sqr_recv)
 
     g_ref[...] = jnp.zeros_like(g_ref)
@@ -164,7 +205,7 @@
 
     def first_gram(c, carry):
         high_high, high_low = carry
-        high, low = split(jnp.concatenate([kb[0, at(c)], ab[0, at(c)]], axis=1))
+        high, low = split(jnp.concatenate([kb[0, load_at(c)], ab[0, load_at(c)]], axis=1))
         return high_high + tdot(high, high), high_low + tdot(high, low)
 
     high_high, high_low = lax.fori_loop(0, CHUNKS, first_gram, (mass_low, mass_low))
@@ -263,6 +304,8 @@
         high, low = split(rotation)
         q_hi[...] = high
         q_lo[...] = low
+        q_src[r] = rotation[:, half:]
+        pass_q(r).start()
 
         @pl.loop(0, CHUNKS)
         def _(c):
@@ -272,9 +315,28 @@
             move(r, c).start()
             kb[r + 1, at(c)] = y[:, :half]
 
+        @pl.loop(0, RAW_BLOCKS)
+        def _(c):
+            high, low = split(jnp.concatenate([kb[r, raw_at(c)], ab[r, raw_at(c)]], axis=1))
+            keep_high, keep_low = q_hi[:, :half], q_lo[:, :half]
+            kb[r + 1, raw_at(c)] = dot(high, keep_high) + (dot(high, keep_low) + dot(low, keep_high))
+
         off = gram * (1.0 - eye)
         tile_row = lax.broadcasted_iota(jnp.int32, off_tile.shape, 0)
         off_tile[...] = jnp.where(tile_row == r, total(off * off), off_tile[...])
+
+        def finish_raw():
+            pass_raw(r, 0).wait()
+            pass_raw(r, 1).wait()
+            pass_q(r).wait()
+
+            @pl.loop(0, RAW_BLOCKS)
+            def _(c):
+                high, low = split(
+                    jnp.concatenate([raw_in[r, 0, raw_at(c)], raw_in[r, 1, raw_at(c)]], axis=1)
+                )
+                move_high, move_low = split(q_in[r])
+                ab[r + 1, raw_at(c)] = dot(high, move_high) + (dot(high, move_low) + dot(low, move_high))
 
         @pl.when(r < ROUNDS - 1)
         def _():
@@ -283,13 +345,24 @@
             pass_mass(r).start()
             g_ref[:half, :half] = mass[:half, :half]
             acc[...] = jnp.zeros_like(acc)
+            finish_raw()
+
+            def cross_gram(where):
+                k_high, k_low = split(kb[r + 1, where])
+                m_high, m_low = split(ab[r + 1, where])
+                acc[...] += tdot(k_high, m_high) + (tdot(k_high, m_low) + tdot(k_low, m_high))
+
+            @pl.loop(0, RAW_BLOCKS)
+            def _(c):
+                cross_gram(raw_at(c))
+
+            pass_raw(r + 1, 0).start()
+            pass_raw(r + 1, 1).start()
 
             @pl.loop(0, CHUNKS)
             def _(c):
-                k_high, k_low = split(kb[r + 1, at(c)])
                 move(r, c).wait()
-                m_high, m_low = split(ab[r + 1, at(c)])
-                acc[...] += tdot(k_high, m_high) + (tdot(k_high, m_low) + tdot(k_low, m_high))
+                cross_gram(at(c))
 
             sendg[r, 0] = acc[...]
             cross = reduce_rows(sendg.at[r], recvg.at[r], r + 1)
@@ -298,12 +371,18 @@
             g_ref[half:, :half] = cross.T
             g_ref[half:, half:] = mass_in[r]
 
+        @pl.when(r == ROUNDS - 1)
+        def _():
+            finish_raw()
+
     off_done = share("pair", pairs, off_tile, off_pairs, off_send, off_recv)
 
     @pl.loop(0, CHUNKS)
     def _(c):
         store(c, 0).start()
 
+    store_raw(0).start()
+    store_raw(1).start()
     off_ref[...] = jnp.sqrt(off_done() / (pairs * width * (width - 1))) / mean_sq
 
     @pl.loop(0, CHUNKS)
@@ -315,6 +394,9 @@
     def _(c):
         store(c, 0).wait()
         store(c, 1).wait()
+
+    store_raw(0).wait()
+    store_raw(1).wait()
 
 
 def local(matrix, plan):
@@ -322,9 +404,10 @@
     half = width // 2
     pairs = lax.axis_size("pair")
     groups = lax.axis_size("rows")
-    if groups & (groups - 1) or rows % (CHUNKS * 8):
+    if groups & (groups - 1) or rows % 1024:
         raise ValueError("sizes")
     stages = groups.bit_length() - 1
+    raw = rows // 8
     dma = pltpu.SemaphoreType.DMA
     tile = (8, 128)
     rotated, off = pl.pallas_call(
@@ -355,8 +438,11 @@
             pltpu.VMEM((pairs,) + tile, F32),
             pltpu.VMEM(tile, F32),
             pltpu.VMEM((pairs,) + tile, F32),
+            pltpu.VMEM((ROUNDS, 2, raw, half), F32),
+            pltpu.VMEM((ROUNDS, width, half), F32),
+            pltpu.VMEM((ROUNDS, width, half), F32),
             dma((2, CHUNKS)),
-            dma((2, CHUNKS)),
+            dma((2, CHUNKS + 1)),
             dma((ROUNDS, CHUNKS)),
             dma((ROUNDS, CHUNKS)),
             dma((ROUNDS, stages)),
@@ -369,6 +455,10 @@
             dma((pairs,)),
             dma((pairs,)),
             dma((pairs,)),
+            dma((ROUNDS, 2)),
+            dma((ROUNDS, 2)),
+            dma((ROUNDS,)),
+            dma((ROUNDS,)),
         ],
         compiler_params=pltpu.CompilerParams(
             collective_id=0, has_side_effects=True, vmem_limit_bytes=50 * 2**20

time: 196 us -> 189 us (0.964)
  Pallas kernels: 189 us -> 183 us
    pallas_call x1, Pallas kernels: 189 us -> 183 us  [local(): pl.pallas_call(functools.partial(kernel, pairs, groups), out_shape=(jax.S...]
where the time goes in v3:
time: 189 us
  Pallas kernels  183 us (97%)
  local copies, waits for them, and re-layouts  5.84 us (3%)
    pallas_call x1, Pallas kernels, local(): pl.pallas_call(functools.partial(kernel, pairs, groups), out_shape=(jax.S...  183 us
    unnamed x2, local copies, waits for them, and re-layouts  5.21 us

profile of v3, /device:TPU:0, one launch (start us, length us, event | category | flops | bytes accessed | tf_op | source)
XLA Modules:
  0.0 189.1 jit_solution(4470740429066538791)
XLA Ops:
  0.6 0.7 copy.5.plan_ref
  1.4 182.6 %shard_map.41 = (f32[4096,256]{1,0:T(8,128)}, f32[8,128]{1,0:T(8,128)S(1)}) custom-call(f32[4096,256]{1,0:T(8,128)} %x_ref.1, s32[3,1]{1,0:T(4,128)S(1)} %copy.5.plan_ref), custom_call_target="tpu_custom_call" | custom-call | tf_op jit(solution)/shard_map/pallas_call | solution.py:413
  184.0 0.6 slice_reduce_fusion
  184.6 4.5 %copy.7 = f32[4096,256]{1,0:T(8,128)} copy(f32[4096,256]{1,0:T(8,128)} %get-tuple-element.8) | data formatting | bytes 8388608

commit v4 on v3

--- a/solution.py
+++ b/solution.py
@@ -461,7 +461,7 @@
             dma((ROUNDS,)),
         ],
         compiler_params=pltpu.CompilerParams(
-            collective_id=0, has_side_effects=True, vmem_limit_bytes=50 * 2**20
+            collective_id=0, has_side_effects=True, vmem_limit_bytes=34 * 2**20
         ),
     )(matrix, plan)
     return rotated, off[:ROUNDS, 0]

time: 189 us -> 188 us (level)
    unnamed x2 -> x4, local copies, waits for them, and re-layouts: 5.21 us -> 4.94 us
where the time goes in v4:
time: 188 us
  Pallas kernels  182 us (97%)
  local copies, waits for them, and re-layouts  5.57 us (3%)
    pallas_call x1, Pallas kernels, local(): pl.pallas_call(functools.partial(kernel, pairs, groups), out_shape=(jax.S...  182 us
    unnamed x4, local copies, waits for them, and re-layouts  4.94 us

profile of v4, /device:TPU:0, one launch (start us, length us, event | category | flops | bytes accessed | tf_op | source)
XLA Modules:
  0.0 188.2 jit_solution(1413787103741222043)
XLA Ops:
  0.6 0.7 copy.5.plan_ref
  1.4 0.0 copy-start
  1.4 2.2 %copy-done = f32[4096,256]{1,0:T(8,128)S(1)} copy-done((f32[4096,256]{1,0:T(8,128)S(1)}, f32[4096,256]{1,0:T(8,128)}, u32[]{:S(2)}) %copy-start) | copy-done | bytes 4194328
  3.6 181.9 %shard_map.41 = (f32[4096,256]{1,0:T(8,128)S(1)}, f32[8,128]{1,0:T(8,128)S(1)}) custom-call(f32[4096,256]{1,0:T(8,128)S(1)} %copy-done, s32[3,1]{1,0:T(4,128)S(1)} %copy.5.plan_ref), custom_call_target="tpu_custom_call" | custom-call | tf_op jit(solution)/shard_map/pallas_call | solution.py:413
  185.5 0.6 slice_reduce_fusion
  186.1 2.0 %copy.7 = f32[4096,256]{1,0:T(8,128)} copy(f32[4096,256]{1,0:T(8,128)S(1)} %get-tuple-element.8) | data formatting | bytes 8388608
Async XLA Ops:
  1.4 2.2 %copy-start = (f32[4096,256]{1,0:T(8,128)S(1)}, f32[4096,256]{1,0:T(8,128)}, u32[]{:S(2)}) copy-start(f32[4096,256]{1,0:T(8,128)} %x_ref.1) | copy-start | bytes 12582916
